TPU v7x, 32 devices: a whole 2x2x4 slice. The times are simulated.
32 devices in a mesh: rep: 4 (over y, x), fsdp: 8 (over z, core).
Axes of the slice: x: 2, y: 2, z: 4, core: 2. Of those that a mesh axis runs over, the one named last changes fastest.
Arguments:
- local_params: float32 [4, 8, 1024, 128], P('rep', None, 'fsdp'), may hold values from -7 to 7
- gradients: bfloat16 [4, 8, 1024, 128], P('rep', None, 'fsdp'), may hold values from -200 to 200
- first_moment: float32 [4, 8, 1024, 128], P('rep', None, 'fsdp'), may hold values from -4 to 4
- second_moment: float32 [4, 8, 1024, 128], P('rep', None, 'fsdp'), may hold values from 0.01 to 1
- global_params: float32 [1024, 128], P('fsdp'), may hold values from -6 to 6
- outer_momentum: float32 [1024, 128], P('fsdp'), may hold values from -6 to 6
- fragment_index: int32 [1], replicated, may hold values from 0 to 7
- step_count: int32 [1], replicated, may hold values from 1 to 16
Outputs:
- local_next: float32 [4, 8, 1024, 128], P('rep', None, 'fsdp')
- first_next: float32 [4, 8, 1024, 128], P('rep', None, 'fsdp')
- second_next: float32 [4, 8, 1024, 128], P('rep', None, 'fsdp')
- global_next: float32 [1024, 128], P('fsdp')
- momentum_next: float32 [1024, 128], P('fsdp')
All inputs are finite; a program needn't handle non-finite values. Where the computation divides by a largest or mean magnitude, that divisor is 1e-20 or more.
Results may differ from a plain program's by a relative error of at most 0.0018.
Values may be sent and summed in bfloat16 or wider, within the bound.
A program may use at most 64 MiB of HBM per device.

v0:
```python
import functools
import math

import jax
import jax.numpy as jnp
from jax import lax
from jax.experimental import pallas as pl
from jax.experimental.pallas import tpu as pltpu
from jax.sharding import PartitionSpec as P

MESH = pl.DeviceIdType.MESH
SUBLANES = 8
SCALE_ROWS = 16


def exchange(
    replicas,
    shards,
    frag_ref,
    step_ref,
    p_hbm,
    g_hbm,
    m_hbm,
    v_hbm,
    gp_hbm,
    om_hbm,
    p_ref,
    g_ref,
    m_ref,
    v_ref,
    coef_ref,
    global_ref,
    momentum_ref,
    gp_ref,
    om_ref,
    coded,
    squares,
    load_sems,
    code_send,
    code_recv,
    square_send,
    square_recv,
    code_credit,
    square_credit,
):
    rep = lax.axis_index("rep")
    shard = lax.axis_index("fsdp")
    rows, cols = gp_ref.shape
    fragments = p_ref.shape[1]

    loads = [
        pltpu.make_async_copy(src, dst, load_sems.at[i])
        for i, (src, dst) in enumerate(
            (
                (g_hbm, g_ref),
                (gp_hbm, gp_ref),
                (p_hbm, p_ref),
                (om_hbm, om_ref),
                (m_hbm, m_ref),
                (v_hbm, v_ref),
            )
        )
    ]

    def higher(index, size, act):
        for k in range(1, size):

            @pl.when(index + k < size)
            def _():
                act(index + k)

    def lower(index, size, act):
        for k in range(size - 1, 0, -1):

            @pl.when(index - k >= 0)
            def _():
                act(index - k)

    def signal(sem, **target):
        pl.semaphore_signal(sem, inc=1, device_id=target, device_id_type=MESH)

    def square_copy(source, target):
        return pltpu.make_async_remote_copy(
            src_ref=squares.at[source],
            dst_ref=squares.at[source],
            send_sem=square_send.at[target],
            recv_sem=square_recv.at[source],
            device_id={"fsdp": target},
            device_id_type=MESH,
        )

    def code_copy(source, target):
        return pltpu.make_async_remote_copy(
            src_ref=coded.at[source],
            dst_ref=coded.at[source],
            send_sem=code_send.at[target],
            recv_sem=code_recv.at[source],
            device_id={"rep": target},
            device_id_type=MESH,
        )

    barrier = pltpu.get_barrier_semaphore()
    for load in loads[:3]:
        load.start()
    higher(shard, shards, lambda i: signal(barrier, fsdp=i))
    higher(rep, replicas, lambda i: signal(barrier, rep=i))

    @pl.when(shard + rep > 0)
    def _():
        pl.semaphore_wait(barrier, shard + rep)

    lower(shard, shards, lambda i: signal(square_credit.at[shard], fsdp=i))
    lower(rep, replicas, lambda i: signal(code_credit.at[rep], rep=i))

    eye = lax.broadcasted_iota(jnp.int32, (cols, cols), 0) == lax.broadcasted_iota(
        jnp.int32, (cols, cols), 1
    )

    loads[0].wait()
    total = jnp.zeros((SUBLANES, cols), jnp.float32)
    for f in range(fragments):
        grad = g_ref[0, f].astype(jnp.float32)
        total = total + jnp.sum((grad * grad).reshape(-1, SUBLANES, cols), axis=0)
    squares[shard] = jnp.sum(total, axis=0, keepdims=True)
    step = jnp.full((SUBLANES, cols), step_ref[0].astype(jnp.float32), jnp.float32)
    coef_ref[1] = 0.1 / (1.0 - jnp.exp(step * math.log(0.9)))
    coef_ref[2] = 1.0 / (1.0 - jnp.exp(step * math.log(0.95)))
    coef_ref[3] = jnp.full((SUBLANES, cols), frag_ref[0].astype(jnp.float32), jnp.float32)
    lower(shard, shards, lambda i: square_copy(shard, i).start())

    for load in loads[1:3]:
        load.wait()
    for load in loads[3:]:
        load.start()
    pseudo = gp_ref[...] - p_ref[0, frag_ref[0]]
    scale = (jnp.max(jnp.abs(pseudo), axis=1, keepdims=True) + 1e-06).astype(jnp.bfloat16)
    scale = scale.astype(jnp.float32)
    coded[rep, :rows] = (pseudo / scale).astype(jnp.bfloat16)
    for c in range(rows // cols):
        column = scale[c * cols : (c + 1) * cols]
        line = jnp.sum(jnp.where(eye, column, 0.0), axis=0, keepdims=True)
        coded[rep, rows + c * SCALE_ROWS : rows + (c + 1) * SCALE_ROWS] = jnp.broadcast_to(
            line, (SCALE_ROWS, cols)
        ).astype(jnp.bfloat16)

    def square_when_heard(i):
        pl.semaphore_wait(square_credit.at[i], 1)
        square_copy(shard, i).start()

    def code_when_heard(i):
        pl.semaphore_wait(code_credit.at[i], 1)
        code_copy(rep, i).start()

    lower(rep, replicas, lambda i: code_copy(rep, i).start())
    higher(rep, replicas, code_when_heard)
    higher(shard, shards, square_when_heard)

    for load in loads[3:]:
        load.wait()

    for k in range(1, replicas):
        source = lax.rem(rep + k, replicas)
        code_copy(source, source).wait_recv()
    for c in range(rows // cols):
        part = slice(c * cols, (c + 1) * cols)
        summed = jnp.zeros((cols, cols), jnp.float32)
        for r in range(replicas):
            line = coded[r, rows + c * SCALE_ROWS : rows + (c + 1) * SCALE_ROWS]
            line = line.astype(jnp.float32)[:1]
            column = jnp.sum(jnp.where(eye, line, 0.0), axis=1, keepdims=True)
            summed = summed + coded[r, part].astype(jnp.float32) * column
        averaged = summed * (1.0 / replicas)
        momentum = 0.9 * om_ref[part] + averaged
        momentum_ref[part] = momentum
        global_ref[part] = gp_ref[part] - 0.7 * (averaged + 0.9 * momentum)

    for k in range(1, shards):
        source = lax.rem(shard + k, shards)
        square_copy(source, source).wait_recv()
    lanes = squares[0]
    for s in range(1, shards):
        lanes = lanes + squares[s]
    square_sum = jnp.broadcast_to(
        jnp.sum(jnp.broadcast_to(lanes, (SUBLANES, cols)), axis=1, keepdims=True),
        (SUBLANES, cols),
    )
    threshold = 0.5 * math.sqrt(fragments * rows * shards * cols)
    coef_ref[0] = jnp.minimum(1.0, threshold * lax.rsqrt(square_sum + 1e-06))

    for k in range(1, shards):
        square_copy(shard, lax.rem(shard + k, shards)).wait_send()
    for k in range(1, replicas):
        code_copy(rep, lax.rem(rep + k, replicas)).wait_send()


def update(
    p_ref,
    g_ref,
    m_ref,
    v_ref,
    coef_ref,
    global_ref,
    momentum_ref,
    p_hbm,
    m_hbm,
    v_hbm,
    global_hbm,
    momentum_hbm,
    p_out,
    m_out,
    v_out,
    outer_sems,
    sems,
):
    outer = [
        pltpu.make_async_copy(global_ref, global_hbm, outer_sems.at[0]),
        pltpu.make_async_copy(momentum_ref, momentum_hbm, outer_sems.at[1]),
    ]
    for copy in outer:
        copy.start()
    clip, rate_one, inv_two, chosen = (coef_ref[i, :1] for i in range(4))
    copies = []
    for f in range(p_ref.shape[1]):
        keep = jnp.where(chosen == f, 0.5, 1.0)
        scaled = g_ref[0, f].astype(jnp.float32) * clip
        first = 0.9 * m_ref[0, f] + 0.1 * scaled
        m_out[0, f] = first
        second = 0.95 * v_ref[0, f] + 0.05 * scaled * scaled
        v_out[0, f] = second
        unbiased = second * inv_two
        root = unbiased * lax.rsqrt(unbiased)
        stepped = 0.99 * p_ref[0, f] - first * rate_one / (root + 1e-08)
        p_out[0, f] = keep * stepped + (1.0 - keep) * global_ref[...]
        for i, (src, dst) in enumerate(((m_out, m_hbm), (v_out, v_hbm), (p_out, p_hbm))):
            copy = pltpu.make_async_copy(src.at[0, f], dst.at[0, f], sems.at[i, f])
            copy.start()
            copies.append(copy)
    for copy in outer + copies:
        copy.wait()


def local(replicas, shards, p, g, m, v, global_params, outer_momentum, fragment_index, step_count):
    rows, cols = global_params.shape
    fragments = p.shape[1]
    f32 = jnp.float32
    hbm = pl.BlockSpec(memory_space=pltpu.HBM)
    vmem = pl.BlockSpec(memory_space=pltpu.VMEM)
    held_rows = rows + rows // cols * SCALE_ROWS
    held = pl.pallas_call(
        functools.partial(exchange, replicas, shards),
        out_shape=(
            pltpu.VMEM(p.shape, p.dtype),
            pltpu.VMEM(g.shape, g.dtype),
            pltpu.VMEM(m.shape, m.dtype),
            pltpu.VMEM(v.shape, v.dtype),
            pltpu.VMEM((4, SUBLANES, cols), f32),
            pltpu.VMEM((rows, cols), f32),
            pltpu.VMEM((rows, cols), f32),
        ),
        in_specs=[pl.BlockSpec(memory_space=pltpu.SMEM)] * 2 + [hbm] * 6,
        out_specs=(vmem,) * 7,
        scratch_shapes=[
            pltpu.VMEM((rows, cols), f32),
            pltpu.VMEM((rows, cols), f32),
            pltpu.VMEM((replicas, held_rows, cols), jnp.bfloat16),
            pltpu.VMEM((shards, 1, cols), f32),
            pltpu.SemaphoreType.DMA((6,)),
            pltpu.SemaphoreType.DMA((replicas,)),
            pltpu.SemaphoreType.DMA((replicas,)),
            pltpu.SemaphoreType.DMA((shards,)),
            pltpu.SemaphoreType.DMA((shards,)),
            pltpu.SemaphoreType.REGULAR((replicas,)),
            pltpu.SemaphoreType.REGULAR((shards,)),
        ],
        compiler_params=pltpu.CompilerParams(
            collective_id=0, has_side_effects=True, vmem_limit_bytes=16 * 1024 * 1024
        ),
        name="exchange",
    )(
        fragment_index,
        step_count,
        *(
            pltpu.with_memory_space_constraint(x, pltpu.HBM)
            for x in (p, g, m, v, global_params, outer_momentum)
        ),
    )
    return pl.pallas_call(
        update,
        out_shape=(
            jax.ShapeDtypeStruct(p.shape, f32),
            jax.ShapeDtypeStruct(m.shape, f32),
            jax.ShapeDtypeStruct(v.shape, f32),
            jax.ShapeDtypeStruct((rows, cols), f32),
            jax.ShapeDtypeStruct((rows, cols), f32),
        ),
        in_specs=[vmem] * 7,
        out_specs=(hbm,) * 5,
        scratch_shapes=[
            pltpu.VMEM(p.shape, f32),
            pltpu.VMEM(m.shape, f32),
            pltpu.VMEM(v.shape, f32),
            pltpu.SemaphoreType.DMA((2,)),
            pltpu.SemaphoreType.DMA((3, fragments)),
        ],
        compiler_params=pltpu.CompilerParams(vmem_limit_bytes=16 * 1024 * 1024),
        name="update",
    )(*held)


def solution(mesh):
    split = P("rep", None, "fsdp", None)
    outer = P("fsdp", None)
    return jax.shard_map(
        functools.partial(local, mesh.shape["rep"], mesh.shape["fsdp"]),
        mesh=mesh,
        in_specs=(split,) * 4 + (outer,) * 2 + (P(),) * 2,
        out_specs=(split,) * 3 + (outer,) * 2,
        check_vma=False,
    )
```

profile of v0, /device:TPU:0, one launch (start us, length us, event | category | flops | bytes accessed | tf_op | source)
XLA Modules:
  0.0 11.5 jit_solution(16118780320631090607)
XLA Ops:
  1.9 8.1 %exchange.1 = (f32[1,8,128,128]{3,2,1,0:T(8,128)S(1)}, bf16[1,8,128,128]{3,2,1,0:T(8,128)(2,1)S(1)}, f32[1,8,128,128]{3,2,1,0:T(8,128)S(1)}, f32[1,8,128,128]{3,...) custom-call(s32[1]{0:T(128)S(6)} %copy.13.frag_ref, ...), custom_call_target="tpu_custom_call" | custom-call | tf_op jit(solution)/shard_map/exchange/pallas_call | solution.py:249
  10.1 1.4 %update.1 = (f32[1,8,128,128]{3,2,1,0:T(8,128)}, f32[1,8,128,128]{3,2,1,0:T(8,128)}, f32[1,8,128,128]{3,2,1,0:T(8,128)}, f32[128,128]{1,0:T(8,128)}, f32[128,128]{1,0:T(8,128)}) custom-call(f32[1,8,128,128]{3,2,1,0:T(8,128)S(1)} %get-tuple-element.12.p_ref, bf16[1,8,128,128]{3,2,1,0:T(8,128)(2,1)S(1)} %get-tuple-element.13.g_ref, ...), custom_call_target="tpu_custom_call" | custom-call | tf_op jit(solution)/shard_map/update/pallas_call | solution.py:287
where the time goes:
time: 11.6 us; the launch traced here: 11.5 us
  Pallas kernels  9.55 us (82%)
  between operations  1.93 us (17%)
    pallas_call x1, Pallas kernels, local(): pl.pallas_call(functools.partial(exchange, replicas, shards), out_shape=(...  8.14 us
    pallas_call x1, Pallas kernels, local(): pl.pallas_call(update, out_shape=(jax.ShapeDtypeStruct(p.shape, f32), jax...  1.41 us

commit v1 on v0

--- a/solution.py
+++ b/solution.py
@@ -13,11 +13,16 @@
 SCALE_ROWS = 16
 
 
+def read(step_ref, said_ref):
+    said_ref[...] = jnp.full(said_ref.shape, step_ref[0].astype(jnp.float32), jnp.float32)
+
+
 def exchange(
     replicas,
     shards,
+    reader,
     frag_ref,
-    step_ref,
+    said_ref,
     p_hbm,
     g_hbm,
     m_hbm,
@@ -116,16 +121,13 @@
         jnp.int32, (cols, cols), 1
     )
 
+    squares[shard, 1:] = said_ref[...]
     loads[0].wait()
     total = jnp.zeros((SUBLANES, cols), jnp.float32)
     for f in range(fragments):
         grad = g_ref[0, f].astype(jnp.float32)
         total = total + jnp.sum((grad * grad).reshape(-1, SUBLANES, cols), axis=0)
-    squares[shard] = jnp.sum(total, axis=0, keepdims=True)
-    step = jnp.full((SUBLANES, cols), step_ref[0].astype(jnp.float32), jnp.float32)
-    coef_ref[1] = 0.1 / (1.0 - jnp.exp(step * math.log(0.9)))
-    coef_ref[2] = 1.0 / (1.0 - jnp.exp(step * math.log(0.95)))
-    coef_ref[3] = jnp.full((SUBLANES, cols), frag_ref[0].astype(jnp.float32), jnp.float32)
+    squares[shard, :1] = jnp.sum(total, axis=0, keepdims=True)
     lower(shard, shards, lambda i: square_copy(shard, i).start())
 
     for load in loads[1:3]:
@@ -155,6 +157,7 @@
     higher(rep, replicas, code_when_heard)
     higher(shard, shards, square_when_heard)
 
+    coef_ref[3] = jnp.full((SUBLANES, cols), frag_ref[0].astype(jnp.float32), jnp.float32)
     for load in loads[3:]:
         load.wait()
 
@@ -174,12 +177,21 @@
         momentum_ref[part] = momentum
         global_ref[part] = gp_ref[part] - 0.7 * (averaged + 0.9 * momentum)
 
-    for k in range(1, shards):
-        source = lax.rem(shard + k, shards)
-        square_copy(source, source).wait_recv()
-    lanes = squares[0]
+    def square_heard(source):
+        @pl.when(shard != source)
+        def _():
+            square_copy(source, source).wait_recv()
+
+    square_heard(reader)
+    step = jnp.broadcast_to(squares[reader, 1:], (SUBLANES, cols))
+    coef_ref[1] = 0.1 / (1.0 - jnp.exp(step * math.log(0.9)))
+    coef_ref[2] = 1.0 / (1.0 - jnp.exp(step * math.log(0.95)))
+    for s in range(shards):
+        if s != reader:
+            square_heard(s)
+    lanes = squares[0, :1]
     for s in range(1, shards):
-        lanes = lanes + squares[s]
+        lanes = lanes + squares[s, :1]
     square_sum = jnp.broadcast_to(
         jnp.sum(jnp.broadcast_to(lanes, (SUBLANES, cols)), axis=1, keepdims=True),
         (SUBLANES, cols),
@@ -246,8 +258,21 @@
     hbm = pl.BlockSpec(memory_space=pltpu.HBM)
     vmem = pl.BlockSpec(memory_space=pltpu.VMEM)
     held_rows = rows + rows // cols * SCALE_ROWS
+    reader = min(1, shards - 1)
+    said = lax.cond(
+        lax.axis_index("fsdp") == reader,
+        pl.pallas_call(
+            read,
+            out_shape=pltpu.VMEM((1, cols), f32),
+            in_specs=[pl.BlockSpec(memory_space=pltpu.SMEM)],
+            out_specs=vmem,
+            name="read",
+        ),
+        lambda _: jnp.zeros((1, cols), f32),
+        step_count,
+    )
     held = pl.pallas_call(
-        functools.partial(exchange, replicas, shards),
+        functools.partial(exchange, replicas, shards, reader),
         out_shape=(
             pltpu.VMEM(p.shape, p.dtype),
             pltpu.VMEM(g.shape, g.dtype),
@@ -257,13 +282,13 @@
             pltpu.VMEM((rows, cols), f32),
             pltpu.VMEM((rows, cols), f32),
         ),
-        in_specs=[pl.BlockSpec(memory_space=pltpu.SMEM)] * 2 + [hbm] * 6,
+        in_specs=[pl.BlockSpec(memory_space=pltpu.SMEM), vmem] + [hbm] * 6,
         out_specs=(vmem,) * 7,
         scratch_shapes=[
             pltpu.VMEM((rows, cols), f32),
             pltpu.VMEM((rows, cols), f32),
             pltpu.VMEM((replicas, held_rows, cols), jnp.bfloat16),
-            pltpu.VMEM((shards, 1, cols), f32),
+            pltpu.VMEM((shards, 2, cols), f32),
             pltpu.SemaphoreType.DMA((6,)),
             pltpu.SemaphoreType.DMA((replicas,)),
             pltpu.SemaphoreType.DMA((replicas,)),
@@ -278,7 +303,7 @@
         name="exchange",
     )(
         fragment_index,
-        step_count,
+        said,
         *(
             pltpu.with_memory_space_constraint(x, pltpu.HBM)
             for x in (p, g, m, v, global_params, outer_momentum)

time: 11.6 us -> 11.1 us (0.957)
  between operations: 1.93 us -> 1.3 us
where the time goes in v1:
time: 11.1 us; the launch traced here: 10.9 us
  Pallas kernels  9.61 us (87%)
  between operations  1.3 us (12%)
    pallas_call x1, Pallas kernels, local(): pl.pallas_call(functools.partial(exchange, replicas, shards, reader), out...  8.21 us
    pallas_call x1, Pallas kernels, local(): pl.pallas_call(update, out_shape=(jax.ShapeDtypeStruct(p.shape, f32), jax...  1.41 us

profile of v1, /device:TPU:0, one launch (start us, length us, event | category | flops | bytes accessed | tf_op | source)
XLA Modules:
  0.0 10.9 jit_solution(6063733551372921941)
XLA Ops:
  1.3 8.2 %exchange.1 = (f32[1,8,128,128]{3,2,1,0:T(8,128)S(1)}, bf16[1,8,128,128]{3,2,1,0:T(8,128)(2,1)S(1)}, f32[1,8,128,128]{3,2,1,0:T(8,128)S(1)}, f32[1,8,128,128]{3,...) custom-call(s32[1]{0:T(128)S(6)} %copy.16.frag_ref, ...), custom_call_target="tpu_custom_call" | custom-call | tf_op jit(solution)/shard_map/exchange/pallas_call | solution.py:274
  9.5 1.4 %update.1 = (f32[1,8,128,128]{3,2,1,0:T(8,128)}, f32[1,8,128,128]{3,2,1,0:T(8,128)}, f32[1,8,128,128]{3,2,1,0:T(8,128)}, f32[128,128]{1,0:T(8,128)}, f32[128,128]{1,0:T(8,128)}) custom-call(f32[1,8,128,128]{3,2,1,0:T(8,128)S(1)} %get-tuple-element.16.p_ref, bf16[1,8,128,128]{3,2,1,0:T(8,128)(2,1)S(1)} %get-tuple-element.17.g_ref, ...), custom_call_target="tpu_custom_call" | custom-call | tf_op jit(solution)/shard_map/update/pallas_call | solution.py:312
  (2 shorter events, 0.0 us)

commit v2 on v1

--- a/solution.py
+++ b/solution.py
@@ -13,15 +13,14 @@
 SCALE_ROWS = 16
 
 
-def read(step_ref, said_ref):
-    said_ref[...] = jnp.full(said_ref.shape, step_ref[0].astype(jnp.float32), jnp.float32)
+def read(scalar_ref, said_ref):
+    said_ref[...] = jnp.full(said_ref.shape, scalar_ref[0].astype(jnp.float32), jnp.float32)
 
 
 def exchange(
     replicas,
     shards,
     reader,
-    frag_ref,
     said_ref,
     p_hbm,
     g_hbm,
@@ -40,6 +39,8 @@
     om_ref,
     coded,
     squares,
+    told_ref,
+    told_sems,
     load_sems,
     code_send,
     code_recv,
@@ -52,6 +53,7 @@
     shard = lax.axis_index("fsdp")
     rows, cols = gp_ref.shape
     fragments = p_ref.shape[1]
+    tells = lax.rem(shard, 2) == 1
 
     loads = [
         pltpu.make_async_copy(src, dst, load_sems.at[i])
@@ -104,6 +106,15 @@
             device_id_type=MESH,
         )
 
+    told_copy = pltpu.make_async_remote_copy(
+        src_ref=said_ref,
+        dst_ref=told_ref,
+        send_sem=told_sems.at[0],
+        recv_sem=told_sems.at[1],
+        device_id={"fsdp": shard + 1 - 2 * lax.rem(shard, 2)},
+        device_id_type=MESH,
+    )
+
     barrier = pltpu.get_barrier_semaphore()
     for load in loads[:3]:
         load.start()
@@ -113,6 +124,11 @@
     @pl.when(shard + rep > 0)
     def _():
         pl.semaphore_wait(barrier, shard + rep)
+
+    @pl.when(tells)
+    def _():
+        told_copy.start()
+        told_ref[...] = said_ref[...]
 
     lower(shard, shards, lambda i: signal(square_credit.at[shard], fsdp=i))
     lower(rep, replicas, lambda i: signal(code_credit.at[rep], rep=i))
@@ -130,11 +146,24 @@
     squares[shard, :1] = jnp.sum(total, axis=0, keepdims=True)
     lower(shard, shards, lambda i: square_copy(shard, i).start())
 
+    def square_when_heard(i):
+        pl.semaphore_wait(square_credit.at[i], 1)
+        square_copy(shard, i).start()
+
+    @pl.when(jnp.logical_not(tells))
+    def _():
+        told_copy.wait_recv()
+
+    told = told_ref[...]
+
     for load in loads[1:3]:
         load.wait()
     for load in loads[3:]:
         load.start()
-    pseudo = gp_ref[...] - p_ref[0, frag_ref[0]]
+    chosen = p_ref[0, 0]
+    for f in range(1, fragments):
+        chosen = jnp.where(told == f, p_ref[0, f], chosen)
+    pseudo = gp_ref[...] - chosen
     scale = (jnp.max(jnp.abs(pseudo), axis=1, keepdims=True) + 1e-06).astype(jnp.bfloat16)
     scale = scale.astype(jnp.float32)
     coded[rep, :rows] = (pseudo / scale).astype(jnp.bfloat16)
@@ -145,10 +174,6 @@
             line, (SCALE_ROWS, cols)
         ).astype(jnp.bfloat16)
 
-    def square_when_heard(i):
-        pl.semaphore_wait(square_credit.at[i], 1)
-        square_copy(shard, i).start()
-
     def code_when_heard(i):
         pl.semaphore_wait(code_credit.at[i], 1)
         code_copy(rep, i).start()
@@ -156,23 +181,25 @@
     lower(rep, replicas, lambda i: code_copy(rep, i).start())
     higher(rep, replicas, code_when_heard)
     higher(shard, shards, square_when_heard)
-
-    coef_ref[3] = jnp.full((SUBLANES, cols), frag_ref[0].astype(jnp.float32), jnp.float32)
+    coef_ref[3] = jnp.broadcast_to(told, (SUBLANES, cols))
     for load in loads[3:]:
         load.wait()
 
-    for k in range(1, replicas):
-        source = lax.rem(rep + k, replicas)
-        code_copy(source, source).wait_recv()
-    for c in range(rows // cols):
-        part = slice(c * cols, (c + 1) * cols)
-        summed = jnp.zeros((cols, cols), jnp.float32)
-        for r in range(replicas):
+    summed = [jnp.zeros((cols, cols), jnp.float32)] * (rows // cols)
+    for r in range(replicas):
+
+        @pl.when(rep != r)
+        def _():
+            code_copy(r, r).wait_recv()
+
+        for c in range(rows // cols):
             line = coded[r, rows + c * SCALE_ROWS : rows + (c + 1) * SCALE_ROWS]
             line = line.astype(jnp.float32)[:1]
             column = jnp.sum(jnp.where(eye, line, 0.0), axis=1, keepdims=True)
-            summed = summed + coded[r, part].astype(jnp.float32) * column
-        averaged = summed * (1.0 / replicas)
+            summed[c] = summed[c] + coded[r, c * cols : (c + 1) * cols].astype(jnp.float32) * column
+    for c in range(rows // cols):
+        part = slice(c * cols, (c + 1) * cols)
+        averaged = summed[c] * (1.0 / replicas)
         momentum = 0.9 * om_ref[part] + averaged
         momentum_ref[part] = momentum
         global_ref[part] = gp_ref[part] - 0.7 * (averaged + 0.9 * momentum)
@@ -203,6 +230,10 @@
         square_copy(shard, lax.rem(shard + k, shards)).wait_send()
     for k in range(1, replicas):
         code_copy(rep, lax.rem(rep + k, replicas)).wait_send()
+
+    @pl.when(tells)
+    def _():
+        told_copy.wait_send()
 
 
 def update(
@@ -258,17 +289,24 @@
     hbm = pl.BlockSpec(memory_space=pltpu.HBM)
     vmem = pl.BlockSpec(memory_space=pltpu.VMEM)
     held_rows = rows + rows // cols * SCALE_ROWS
-    reader = min(1, shards - 1)
-    said = lax.cond(
-        lax.axis_index("fsdp") == reader,
-        pl.pallas_call(
-            read,
-            out_shape=pltpu.VMEM((1, cols), f32),
-            in_specs=[pl.BlockSpec(memory_space=pltpu.SMEM)],
-            out_specs=vmem,
-            name="read",
-        ),
-        lambda _: jnp.zeros((1, cols), f32),
+    assert shards % 2 == 0
+    reader = 2 % shards
+    shard = lax.axis_index("fsdp")
+    speak = pl.pallas_call(
+        read,
+        out_shape=pltpu.VMEM((1, cols), f32),
+        in_specs=[pl.BlockSpec(memory_space=pltpu.SMEM)],
+        out_specs=vmem,
+        name="read",
+    )
+    said = lax.switch(
+        jnp.where(shard % 2 == 1, 0, jnp.where(shard == reader, 1, 2)),
+        (
+            lambda frag, step: speak(frag),
+            lambda frag, step: speak(step),
+            lambda frag, step: jnp.zeros((1, cols), f32),
+        ),
+        fragment_index,
         step_count,
     )
     held = pl.pallas_call(
@@ -282,13 +320,15 @@
             pltpu.VMEM((rows, cols), f32),
             pltpu.VMEM((rows, cols), f32),
         ),
-        in_specs=[pl.BlockSpec(memory_space=pltpu.SMEM), vmem] + [hbm] * 6,
+        in_specs=[vmem] + [hbm] * 6,
         out_specs=(vmem,) * 7,
         scratch_shapes=[
             pltpu.VMEM((rows, cols), f32),
             pltpu.VMEM((rows, cols), f32),
             pltpu.VMEM((replicas, held_rows, cols), jnp.bfloat16),
             pltpu.VMEM((shards, 2, cols), f32),
+            pltpu.VMEM((1, cols), f32),
+            pltpu.SemaphoreType.DMA((2,)),
             pltpu.SemaphoreType.DMA((6,)),
             pltpu.SemaphoreType.DMA((replicas,)),
             pltpu.SemaphoreType.DMA((replicas,)),
@@ -302,7 +342,6 @@
         ),
         name="exchange",
     )(
-        fragment_index,
         said,
         *(
             pltpu.with_memory_space_constraint(x, pltpu.HBM)

time: 11.1 us -> 10.7 us (0.964)
  between operations: 1.3 us -> 0.67 us
  Pallas kernels: 9.61 us -> 9.87 us
    pallas_call x1, Pallas kernels: 8.21 us -> 8.46 us  [local(): pl.pallas_call(functools.partial(exchange, replicas, shards, reader), out...]
where the time goes in v2:
time: 10.7 us; the launch traced here: 10.6 us
  Pallas kernels  9.87 us (92%)
  between operations  0.67 us (6%)
    pallas_call x1, Pallas kernels, local(): pl.pallas_call(functools.partial(exchange, replicas, shards, reader), out...  8.46 us
    pallas_call x1, Pallas kernels, local(): pl.pallas_call(update, out_shape=(jax.ShapeDtypeStruct(p.shape, f32), jax...  1.41 us

profile of v2, /device:TPU:0, one launch (start us, length us, event | category | flops | bytes accessed | tf_op | source)
XLA Modules:
  0.0 10.6 jit_solution(8070736418178855087)
XLA Ops:
  0.7 8.5 %exchange.1 = (f32[1,8,128,128]{3,2,1,0:T(8,128)S(1)}, bf16[1,8,128,128]{3,2,1,0:T(8,128)(2,1)S(1)}, f32[1,8,128,128]{3,2,1,0:T(8,128)S(1)}, f32[1,8,128,128]{3,...) custom-call(f32[1,128]{1,0:T(1,128)S(1)} %get-tuple-element.29.said_ref, ...), custom_call_target="tpu_custom_call" | custom-call | tf_op jit(solution)/shard_map/exchange/pallas_call | solution.py:312
  9.2 1.4 %update.1 = (f32[1,8,128,128]{3,2,1,0:T(8,128)}, f32[1,8,128,128]{3,2,1,0:T(8,128)}, f32[1,8,128,128]{3,2,1,0:T(8,128)}, f32[128,128]{1,0:T(8,128)}, f32[128,128]{1,0:T(8,128)}) custom-call(f32[1,8,128,128]{3,2,1,0:T(8,128)S(1)} %get-tuple-element.18.p_ref, bf16[1,8,128,128]{3,2,1,0:T(8,128)(2,1)S(1)} %get-tuple-element.19.g_ref, ...), custom_call_target="tpu_custom_call" | custom-call | tf_op jit(solution)/shard_map/update/pallas_call | solution.py:351
  (2 shorter events, 0.0 us)

commit v3 on v2

--- a/solution.py
+++ b/solution.py
@@ -53,6 +53,7 @@
     shard = lax.axis_index("fsdp")
     rows, cols = gp_ref.shape
     fragments = p_ref.shape[1]
+    pair = shard // 2
     tells = lax.rem(shard, 2) == 1
 
     loads = [
@@ -90,8 +91,8 @@
         return pltpu.make_async_remote_copy(
             src_ref=squares.at[source],
             dst_ref=squares.at[source],
-            send_sem=square_send.at[target],
-            recv_sem=square_recv.at[source],
+            send_sem=square_send,
+            recv_sem=square_recv,
             device_id={"fsdp": target},
             device_id_type=MESH,
         )
@@ -100,7 +101,7 @@
         return pltpu.make_async_remote_copy(
             src_ref=coded.at[source],
             dst_ref=coded.at[source],
-            send_sem=code_send.at[target],
+            send_sem=code_send,
             recv_sem=code_recv.at[source],
             device_id={"rep": target},
             device_id_type=MESH,
@@ -130,8 +131,8 @@
         told_copy.start()
         told_ref[...] = said_ref[...]
 
-    lower(shard, shards, lambda i: signal(square_credit.at[shard], fsdp=i))
-    lower(rep, replicas, lambda i: signal(code_credit.at[rep], rep=i))
+    lower(shard, shards, lambda i: signal(square_credit.at[pair], fsdp=i))
+    lower(rep, replicas, lambda i: signal(code_credit, rep=i))
 
     eye = lax.broadcasted_iota(jnp.int32, (cols, cols), 0) == lax.broadcasted_iota(
         jnp.int32, (cols, cols), 1
@@ -145,10 +146,6 @@
         total = total + jnp.sum((grad * grad).reshape(-1, SUBLANES, cols), axis=0)
     squares[shard, :1] = jnp.sum(total, axis=0, keepdims=True)
     lower(shard, shards, lambda i: square_copy(shard, i).start())
-
-    def square_when_heard(i):
-        pl.semaphore_wait(square_credit.at[i], 1)
-        square_copy(shard, i).start()
 
     @pl.when(jnp.logical_not(tells))
     def _():
@@ -174,13 +171,25 @@
             line, (SCALE_ROWS, cols)
         ).astype(jnp.bfloat16)
 
-    def code_when_heard(i):
-        pl.semaphore_wait(code_credit.at[i], 1)
-        code_copy(rep, i).start()
-
     lower(rep, replicas, lambda i: code_copy(rep, i).start())
-    higher(rep, replicas, code_when_heard)
-    higher(shard, shards, square_when_heard)
+
+    @pl.when(rep + 1 < replicas)
+    def _():
+        pl.semaphore_wait(code_credit, replicas - 1 - rep)
+
+    higher(rep, replicas, lambda i: code_copy(rep, i).start())
+
+    @pl.when(jnp.logical_not(tells))
+    def _():
+        pl.semaphore_wait(square_credit.at[pair], 1)
+        square_copy(shard, shard + 1).start()
+
+    def squares_when_heard(chip):
+        pl.semaphore_wait(square_credit.at[chip], 2)
+        square_copy(shard, 2 * chip).start()
+        square_copy(shard, 2 * chip + 1).start()
+
+    higher(pair, shards // 2, squares_when_heard)
     coef_ref[3] = jnp.broadcast_to(told, (SUBLANES, cols))
     for load in loads[3:]:
         load.wait()
@@ -204,18 +213,11 @@
         momentum_ref[part] = momentum
         global_ref[part] = gp_ref[part] - 0.7 * (averaged + 0.9 * momentum)
 
-    def square_heard(source):
-        @pl.when(shard != source)
-        def _():
-            square_copy(source, source).wait_recv()
-
-    square_heard(reader)
+    others = squares.at[pl.ds(0, shards - 1)]
+    pltpu.make_async_copy(others, others, square_recv).wait()
     step = jnp.broadcast_to(squares[reader, 1:], (SUBLANES, cols))
     coef_ref[1] = 0.1 / (1.0 - jnp.exp(step * math.log(0.9)))
     coef_ref[2] = 1.0 / (1.0 - jnp.exp(step * math.log(0.95)))
-    for s in range(shards):
-        if s != reader:
-            square_heard(s)
     lanes = squares[0, :1]
     for s in range(1, shards):
         lanes = lanes + squares[s, :1]
@@ -226,10 +228,9 @@
     threshold = 0.5 * math.sqrt(fragments * rows * shards * cols)
     coef_ref[0] = jnp.minimum(1.0, threshold * lax.rsqrt(square_sum + 1e-06))
 
-    for k in range(1, shards):
-        square_copy(shard, lax.rem(shard + k, shards)).wait_send()
-    for k in range(1, replicas):
-        code_copy(rep, lax.rem(rep + k, replicas)).wait_send()
+    pltpu.make_async_copy(others, others, square_send).wait()
+    sent = coded.at[pl.ds(0, replicas - 1)]
+    pltpu.make_async_copy(sent, sent, code_send).wait()
 
     @pl.when(tells)
     def _():
@@ -262,7 +263,6 @@
     for copy in outer:
         copy.start()
     clip, rate_one, inv_two, chosen = (coef_ref[i, :1] for i in range(4))
-    copies = []
     for f in range(p_ref.shape[1]):
         keep = jnp.where(chosen == f, 0.5, 1.0)
         scaled = g_ref[0, f].astype(jnp.float32) * clip
@@ -275,10 +275,11 @@
         stepped = 0.99 * p_ref[0, f] - first * rate_one / (root + 1e-08)
         p_out[0, f] = keep * stepped + (1.0 - keep) * global_ref[...]
         for i, (src, dst) in enumerate(((m_out, m_hbm), (v_out, v_hbm), (p_out, p_hbm))):
-            copy = pltpu.make_async_copy(src.at[0, f], dst.at[0, f], sems.at[i, f])
+            copy = pltpu.make_async_copy(src.at[0, f], dst.at[0, f], sems.at[i])
             copy.start()
-            copies.append(copy)
-    for copy in outer + copies:
+    for i, (src, dst) in enumerate(((m_out, m_hbm), (v_out, v_hbm), (p_out, p_hbm))):
+        pltpu.make_async_copy(src, dst, sems.at[i]).wait()
+    for copy in outer:
         copy.wait()
 
 
@@ -330,12 +331,12 @@
             pltpu.VMEM((1, cols), f32),
             pltpu.SemaphoreType.DMA((2,)),
             pltpu.SemaphoreType.DMA((6,)),
+            pltpu.SemaphoreType.DMA,
             pltpu.SemaphoreType.DMA((replicas,)),
-            pltpu.SemaphoreType.DMA((replicas,)),
-            pltpu.SemaphoreType.DMA((shards,)),
-            pltpu.SemaphoreType.DMA((shards,)),
-            pltpu.SemaphoreType.REGULAR((replicas,)),
-            pltpu.SemaphoreType.REGULAR((shards,)),
+            pltpu.SemaphoreType.DMA,
+            pltpu.SemaphoreType.DMA,
+            pltpu.SemaphoreType.REGULAR,
+            pltpu.SemaphoreType.REGULAR((shards // 2,)),
         ],
         compiler_params=pltpu.CompilerParams(
             collective_id=0, has_side_effects=True, vmem_limit_bytes=16 * 1024 * 1024
@@ -364,7 +365,7 @@
             pltpu.VMEM(m.shape, f32),
             pltpu.VMEM(v.shape, f32),
             pltpu.SemaphoreType.DMA((2,)),
-            pltpu.SemaphoreType.DMA((3, fragments)),
+            pltpu.SemaphoreType.DMA((3,)),
         ],
         compiler_params=pltpu.CompilerParams(vmem_limit_bytes=16 * 1024 * 1024),
         name="update",

time: 10.7 us -> 10.3 us (0.963)
  Pallas kernels: 9.87 us -> 9.43 us
    pallas_call x1, Pallas kernels: 8.46 us -> 8.21 us  [local(): pl.pallas_call(functools.partial(exchange, replicas, shards, reader), out...]
    pallas_call x1, Pallas kernels: 1.41 us -> 1.22 us  [local(): pl.pallas_call(update, out_shape=(jax.ShapeDtypeStruct(p.shape, f32), jax...]
where the time goes in v3:
time: 10.3 us; the launch traced here: 10.1 us
  Pallas kernels  9.43 us (92%)
  between operations  0.67 us (7%)
    pallas_call x1, Pallas kernels, local(): pl.pallas_call(functools.partial(exchange, replicas, shards, reader), out...  8.21 us
    pallas_call x1, Pallas kernels, local(): pl.pallas_call(update, out_shape=(jax.ShapeDtypeStruct(p.shape, f32), jax...  1.22 us

profile of v3, /device:TPU:0, one launch (start us, length us, event | category | flops | bytes accessed | tf_op | source)
XLA Modules:
  0.0 10.1 jit_solution(10479918371881307665)
XLA Ops:
  0.7 8.2 %exchange.1 = (f32[1,8,128,128]{3,2,1,0:T(8,128)S(1)}, bf16[1,8,128,128]{3,2,1,0:T(8,128)(2,1)S(1)}, f32[1,8,128,128]{3,2,1,0:T(8,128)S(1)}, f32[1,8,128,128]{3,...) custom-call(f32[1,128]{1,0:T(1,128)S(1)} %get-tuple-element.29.said_ref, ...), custom_call_target="tpu_custom_call" | custom-call | tf_op jit(solution)/shard_map/exchange/pallas_call | solution.py:313
  8.9 1.2 %update.1 = (f32[1,8,128,128]{3,2,1,0:T(8,128)}, f32[1,8,128,128]{3,2,1,0:T(8,128)}, f32[1,8,128,128]{3,2,1,0:T(8,128)}, f32[128,128]{1,0:T(8,128)}, f32[128,128]{1,0:T(8,128)}) custom-call(f32[1,8,128,128]{3,2,1,0:T(8,128)S(1)} %get-tuple-element.18.p_ref, bf16[1,8,128,128]{3,2,1,0:T(8,128)(2,1)S(1)} %get-tuple-element.19.g_ref, ...), custom_call_target="tpu_custom_call" | custom-call | tf_op jit(solution)/shard_map/update/pallas_call | solution.py:352
  (2 shorter events, 0.0 us)
